TPU v7x, 512 devices: a whole 4x8x8 slice. The times are simulated.
512 devices in a mesh: shard: 64 (over x, z, core), rep: 8 (over y).
Axes of the slice: x: 4, y: 8, z: 8, core: 2. Of those that a mesh axis runs over, the one named last changes fastest.
Arguments:
- attn_grad: bfloat16 [8, 2, 4, 768, 768], P('rep', None, None, 'shard'), may hold values from -16 to 16
- attn_error: float32 [8, 2, 4, 768, 768], P('rep', None, None, 'shard'), may hold values from -6 to 6
- attn_basis: float32 [2, 4, 768, 32], P(None, None, 'shard'), may hold values from -0.21875 to 0.21875
- attn_roots: float32 [2, 4, 3, 32, 32], replicated, as said below
- attn_momentum: float32 [2, 4, 768, 768], P(None, None, 'shard'), may hold values from -4 to 4
- attn_weights: float32 [2, 4, 768, 768], P(None, None, 'shard'), may hold values from -0.21875 to 0.21875
- mlp_grad: bfloat16 [8, 2, 2, 768, 3072], P('rep', None, None, 'shard'), may hold values from -16 to 16
- mlp_error: float32 [8, 2, 2, 768, 3072], P('rep', None, None, 'shard'), may hold values from -6 to 6
- mlp_basis: float32 [2, 2, 3072, 32], P(None, None, 'shard'), may hold values from -0.109375 to 0.109375
- mlp_roots: float32 [2, 2, 3, 32, 32], replicated, as said below
- mlp_momentum: float32 [2, 2, 768, 3072], P(None, None, 'shard'), may hold values from -4 to 4
- mlp_weights: float32 [2, 2, 768, 3072], P(None, None, 'shard'), may hold values from -0.21875 to 0.21875
- small_grad: bfloat16 [8, 2, 9984], P('rep', None, 'shard'), may hold values from -6 to 6
- small_momentum: float32 [2, 9984], P(None, 'shard'), may hold values from -4 to 4
- small_weights: float32 [2, 9984], P(None, 'shard'), may hold values from -6 to 6
Outputs:
- attn_error_out: float32 [8, 2, 4, 768, 768], P('rep', None, None, 'shard')
- mlp_error_out: float32 [8, 2, 2, 768, 3072], P('rep', None, None, 'shard')
- attn_left: float32 [2, 4, 768, 32], P(None, None, 'shard')
- attn_right: float32 [2, 4, 768, 32], P(None, None, 'shard')
- mlp_left: float32 [2, 2, 768, 32], P(None, None, 'shard')
- mlp_right: float32 [2, 2, 3072, 32], P(None, None, 'shard')
- attn_momentum_out: float32 [2, 4, 768, 768], P(None, None, 'shard')
- attn_weights_out: float32 [2, 4, 768, 768], P(None, None, 'shard')
- mlp_momentum_out: float32 [2, 2, 768, 3072], P(None, None, 'shard')
- mlp_weights_out: float32 [2, 2, 768, 3072], P(None, None, 'shard')
- small_momentum_out: float32 [2, 9984], P(None, 'shard')
- small_weights_out: float32 [2, 9984], P(None, 'shard')
Inputs may be any that keep to these rules, and one draw needn't show every extreme that they name: Every 32 x 32 factor of attn_roots is a scaled identity plus independent entries and is well conditioned. Every 32 x 32 factor of mlp_roots is a scaled identity plus independent entries and is well conditioned.
All inputs are finite; a program needn't handle non-finite values.
Results may differ from a plain program's by a relative error of at most 0.0003.
Values sent between devices are 32-bit elements; how exact they have to be, the bound alone decides.
A program may use at most 64 MiB of HBM per device.

v0:
```python
import jax
import jax.numpy as jnp
from jax import lax
from jax.sharding import PartitionSpec as P

momentum_decay = 0.9
learn_rate = 0.05


def rows_product(merged, factor):
    return jnp.einsum("lkrc,lkcn->lkrn", merged, factor, precision=lax.Precision.HIGHEST)


def cols_product(merged, factor):
    return jnp.einsum("lkrc,lkrn->lkcn", merged, factor, precision=lax.Precision.HIGHEST)


def rotate(factor, inverse_roots, round_index):
    return jnp.einsum(
        "lkrn,lknm->lkrm", factor, inverse_roots[:, :, round_index], precision=lax.Precision.HIGHEST
    )


def finish(summed, inverse_roots, round_index):
    if round_index < 0:
        return summed / float(lax.axis_size("rep"))
    return rotate(summed, inverse_roots, round_index)


def own_share(full_factor):
    share_width = full_factor.shape[2] // lax.axis_size("shard")
    share_start = lax.axis_index("shard") * share_width
    return lax.dynamic_slice_in_dim(full_factor, share_start, share_width, 2)


def column_round(attn_term, mlp_term, attn_roots, mlp_roots, round_index):
    attn_full, mlp_full = lax.psum((attn_term, mlp_term), ("shard", "rep"))
    attn_full = finish(attn_full, attn_roots, round_index)
    mlp_full = finish(mlp_full, mlp_roots, round_index)
    attn_share = own_share(attn_full)
    mlp_share = own_share(mlp_full)
    attn_next, mlp_next = (attn_full, mlp_full)
    return (attn_next, mlp_next, attn_full, mlp_full, attn_share, mlp_share)


def update(merged, approx, momentum, weights):
    error_out = (merged - approx)[None]
    momentum_out = momentum_decay * momentum + approx
    weights_out = weights - learn_rate * momentum_out
    return (error_out, momentum_out, weights_out)


def per_device(
    attn_grad,
    attn_error,
    attn_basis,
    attn_roots,
    attn_momentum,
    attn_weights,
    mlp_grad,
    mlp_error,
    mlp_basis,
    mlp_roots,
    mlp_momentum,
    mlp_weights,
    small_grad,
    small_momentum,
    small_weights,
):
    attn_merged = attn_grad[0].astype(jnp.float32) + attn_error[0]
    mlp_merged = mlp_grad[0].astype(jnp.float32) + mlp_error[0]
    small_local = small_grad[0].astype(jnp.float32)
    attn_bfull, mlp_bfull = (
        lax.all_gather(attn_basis, "shard", axis=2, tiled=True),
        lax.all_gather(mlp_basis, "shard", axis=2, tiled=True),
    )
    attn_data, mlp_data = (attn_merged, mlp_merged)
    attn_start, mlp_start = (attn_bfull, mlp_bfull)
    attn_first = rows_product(attn_data, attn_start)
    mlp_first = rows_product(mlp_data, mlp_start)
    small_total = lax.psum(small_local, "rep")
    attn_first, mlp_first = lax.psum((attn_first, mlp_first), "rep")
    attn_lhat = rotate(attn_first, attn_roots, 0)
    mlp_lhat = rotate(mlp_first, mlp_roots, 0)
    attn_rhat, mlp_rhat, spare_one, spare_two, spare_three, spare_four = column_round(
        cols_product(attn_data, attn_lhat),
        cols_product(mlp_data, mlp_lhat),
        attn_roots,
        mlp_roots,
        1,
    )
    attn_second, mlp_second = lax.psum(
        (rows_product(attn_data, attn_rhat), rows_product(mlp_data, mlp_rhat)), "rep"
    )
    attn_left = rotate(attn_second, attn_roots, 2)
    mlp_left = rotate(mlp_second, mlp_roots, 2)
    spare_five, spare_six, attn_rfull, mlp_rfull, attn_right, mlp_right = column_round(
        cols_product(attn_data, attn_left),
        cols_product(mlp_data, mlp_left),
        attn_roots,
        mlp_roots,
        -1,
    )
    attn_approx = jnp.einsum(
        "lkrn,lkcn->lkrc", attn_left, attn_rfull, precision=lax.Precision.HIGHEST
    )
    mlp_approx = jnp.einsum("lkrn,lkcn->lkrc", mlp_left, mlp_rfull, precision=lax.Precision.HIGHEST)
    attn_error_out, attn_momentum_out, attn_weights_out = update(
        attn_merged, attn_approx, attn_momentum, attn_weights
    )
    mlp_error_out, mlp_momentum_out, mlp_weights_out = update(
        mlp_merged, mlp_approx, mlp_momentum, mlp_weights
    )
    small_mean = small_total / float(lax.axis_size("rep"))
    small_momentum_out = momentum_decay * small_momentum + small_mean
    small_weights_out = small_weights - learn_rate * small_momentum_out
    return (
        attn_error_out,
        mlp_error_out,
        attn_left,
        attn_right,
        mlp_left,
        mlp_right,
        attn_momentum_out,
        attn_weights_out,
        mlp_momentum_out,
        mlp_weights_out,
        small_momentum_out,
        small_weights_out,
    )


def solution(mesh):
    in_specs = (
        P("rep", None, None, "shard", None),
        P("rep", None, None, "shard", None),
        P(None, None, "shard", None),
        P(),
        P(None, None, "shard", None),
        P(None, None, "shard", None),
        P("rep", None, None, "shard", None),
        P("rep", None, None, "shard", None),
        P(None, None, "shard", None),
        P(),
        P(None, None, "shard", None),
        P(None, None, "shard", None),
        P("rep", None, "shard"),
        P(None, "shard"),
        P(None, "shard"),
    )
    out_specs = (
        P("rep", None, None, "shard", None),
        P("rep", None, None, "shard", None),
        P(None, None, "shard", None),
        P(None, None, "shard", None),
        P(None, None, "shard", None),
        P(None, None, "shard", None),
        P(None, None, "shard", None),
        P(None, None, "shard", None),
        P(None, None, "shard", None),
        P(None, None, "shard", None),
        P(None, "shard"),
        P(None, "shard"),
    )
    return jax.shard_map(
        per_device, mesh=mesh, in_specs=in_specs, out_specs=out_specs, check_vma=False
    )
```

profile of v0, /device:TPU:1, one launch (start us, length us, event | category | flops | bytes accessed | tf_op | source)
XLA Modules:
  0.0 757.0 jit_solution(16800400785792100691)
XLA Ops:
  7.2 1.6 copy.101
  8.9 0.8 copy.94
  9.7 59.7 %all_gather.6 = f32[2,4,768,32]{3,1,0,2:T(4,128)S(1)} all-gather(f32[2,4,12,32]{3,1,0,2:T(4,128)S(1)} %copy.94), channel_id=1, replica_groups=mesh['shard'=64,'rep'=8] {'shard'}, dimensions={2}, use_global_device_ids=true | all-gather | bytes 798720 | tf_op jit(solution)/shard_map/all_gather | solution.py:74
  69.4 2.1 fusion.2
  71.6 33.6 %all-gather.2.cloned.1.call-done = f32[2,2,3072,32]{3,1,0,2:T(2,128)} async-done(((f32[2,2,48,32]{3,1,0,2:T(2,128)}), f32[2,2,3072,32]{3,1,0,2:T(2,128)}) %all-gather.2.cloned.1.call-update) | async-done | bytes 1572880 | tf_op jit(solution)/shard_map/all_gather | solution.py:75
  105.2 6.1 fusion
  111.3 23.7 %all-reduce.3 = (f32[2,4,12,32]{3,2,1,0:T(8,128)S(1)}, f32[2,2,12,32]{3,2,1,0:T(8,128)S(1)}) all-reduce(f32[2,4,12,32]{3,2,1,0:T(8,128)S(1)} %fusion.2, f32[2,2,12,32]{3,2,1,0:T(8,128)S(1)} %fusion), channel_id=1, replica_groups=mesh['shard'=64,'rep'=8] {'rep'}, use_global_device_ids=true, to_apply=%region_0.0 | all-reduce | flops 4608 | bytes 36864 | tf_op jit(solution)/shard_map/psum | solution.py:82
  135.3 1.7 fusion.17
  137.2 2.8 fusion.8
  140.7 279.9 %all-reduce.9.cloned.1.call-done = (f32[2,4,768,32]{2,3,1,0:T(8,128)}, f32[2,2,3072,32]{2,3,1,0:T(8,128)}) async-done(((f32[2,4,768,32]{2,3,1,0:T(8,128)}, f32[2,2,3072,32]{2,3,1,0:T(8,128)}), (f32[2,4,768,32]{2,3,1,0:T(8,128)}, f32[2,2,3072,32]{2,3,1,0:T(8,128)})) %all-reduce.9.cloned.1.call-update) | async-done | bytes 2359312 | tf_op jit(solution)/shard_map/psum | solution.py:37
  420.6 2.1 fusion.22
  422.7 0.8 fusion.15
  423.5 1.5 fusion.31
  424.9 1.6 fusion.6
  426.6 23.4 %all-reduce.2 = (f32[2,4,12,32]{3,2,1,0:T(8,128)S(1)}, f32[2,2,12,32]{3,2,1,0:T(8,128)S(1)}, f32[2,156]{1,0:T(2,128)S(1)}) all-reduce(f32[2,4,12,32]{3,2,1,0:T(8,128)S(1)} %fusion.15, f32[2,2,12,32]{3,2,1,0:T(8,128)S(1)} %fusion.6, f32[2,156]{1,0:T(2,128)S(1)} %bitcast_convert_fusion), channel_id=1, replica_groups=mesh['shard'=64,'rep'=8] {'rep'}, use_global_device_ids=true, to_apply=%region_2.0 | all-reduce | flops 4920 | bytes 39360 | tf_op jit(solution)/shard_map/psum | solution.py:92
  450.4 1.7 fusion.13
  452.1 2.8 fusion.4
  454.9 0.6 copy.114
  455.6 0.6 copy.112
  456.8 280.8 %all-reduce.7.cloned.1.call-done = (f32[2,4,768,32]{2,3,1,0:T(8,128)}, f32[2,2,3072,32]{2,3,1,0:T(8,128)}) async-done(((f32[2,4,768,32]{2,3,1,0:T(8,128)}, f32[2,2,3072,32]{2,3,1,0:T(8,128)}), (f32[2,4,768,32]{2,3,1,0:T(8,128)}, f32[2,2,3072,32]{2,3,1,0:T(8,128)})) %all-reduce.7.cloned.1.call-update) | async-done | bytes 2359312 | tf_op jit(solution)/shard_map/psum | solution.py:37
  737.6 1.3 broadcast_multiply_fusion.1
  739.0 0.7 copy.113
  739.7 0.7 copy_subtract_fusion.1
  740.4 0.9 copy.116
  741.3 0.9 copy.115
  742.2 0.9 copy.110
  743.3 0.9 copy-done.7
  744.4 1.5 copy_subtract_fusion
  745.9 1.3 copy.118
  747.2 1.3 copy.117
  748.5 1.3 copy.111
  749.7 0.7 constant_dynamic-slice_fusion
  (45 shorter events, 2.7 us)
Async XLA Ops:
  7.2 98.0 %all-gather.2.cloned.1.call-start = ((), (), s32[]{:S(2)}) async-start(), calls=%async_computation | async-start | bytes 6389760 | tf_op jit(solution)/shard_map/all_gather | solution.py:75
  8.8 411.8 %all-reduce.9.cloned.1.call-start = ((), (), s32[]{:S(2)}) async-start(), calls=%async_computation.2 | async-start | bytes 4718592 | tf_op jit(solution)/shard_map/psum | solution.py:37
  9.7 59.7 %copy-start.2 = (f32[1,2,4,12,768]{4,2,3,1,0:T(4,128)S(1)}, f32[1,2,4,12,768]{4,2,3,1,0:T(4,128)}, u32[]{:S(2)}) copy-start(f32[1,2,4,12,768]{4,2,3,1,0:T(4,128)} %param.16) | copy-start | bytes 884740
  9.7 59.7 %copy-start.3 = (bf16[1,2,4,12,768]{4,2,3,1,0:T(4,128)(2,1)S(1)}, bf16[1,2,4,12,768]{4,2,3,1,0:T(4,128)(2,1)}, u32[]{:S(2)}) copy-start(bf16[1,2,4,12,768]{4,2,3,1,0:T(4,128)(2,1)} %param.15) | copy-start | bytes 442372
  69.4 35.8 %copy-start = (f32[1,2,2,12,3072]{4,2,3,1,0:T(2,128)S(1)}, f32[1,2,2,12,3072]{4,2,3,1,0:T(2,128)}, u32[]{:S(2)}) copy-start(f32[1,2,2,12,3072]{4,2,3,1,0:T(2,128)} %param.22) | copy-start | bytes 1769476
  69.4 35.8 %copy-start.1 = (bf16[1,2,2,12,3072]{4,2,3,1,0:T(2,128)(2,1)S(1)}, bf16[1,2,2,12,3072]{4,2,3,1,0:T(2,128)(2,1)}, u32[]{:S(2)}) copy-start(bf16[1,2,2,12,3072]{4,2,3,1,0:T(2,128)(2,1)} %param.21) | copy-start | bytes 884740
  71.5 63.5 %copy-start.11 = (f32[2,4,3,32,32]{4,3,2,1,0:T(8,128)S(1)}, f32[2,4,3,32,32]{4,3,2,1,0:T(8,128)}, u32[]{:S(2)}) copy-start(f32[2,4,3,32,32]{4,3,2,1,0:T(8,128)} %param.18) | copy-start | bytes 294916
  111.3 25.7 %copy-start.12 = (f32[2,2,3,32,32]{4,3,2,1,0:T(8,128)S(1)}, f32[2,2,3,32,32]{4,3,2,1,0:T(8,128)}, u32[]{:S(2)}) copy-start(f32[2,2,3,32,32]{4,3,2,1,0:T(8,128)} %param.24) | copy-start | bytes 147460
  140.0 0.7 copy-start.15
  140.0 597.6 %all-reduce.7.cloned.1.call-start = ((), (), s32[]{:S(2)}) async-start(), calls=%async_computation.1 | async-start | bytes 4718592 | tf_op jit(solution)/shard_map/psum | solution.py:37
  420.6 2.9 copy-start.6
  454.9 1.3 copy-start.13
  454.9 1.3 copy-start.14
  454.9 284.8 %copy-start.9 = (f32[2,4,12,768]{3,1,2,0:T(4,128)S(1)}, f32[2,4,12,768]{3,1,2,0:T(4,128)}, u32[]{:S(2)}) copy-start(f32[2,4,12,768]{3,1,2,0:T(4,128)} %param.20) | copy-start | bytes 884740
  454.9 284.8 %copy-start.10 = (f32[2,4,12,768]{3,1,2,0:T(4,128)S(1)}, f32[2,4,12,768]{3,1,2,0:T(4,128)}, u32[]{:S(2)}) copy-start(f32[2,4,12,768]{3,1,2,0:T(4,128)} %param.19) | copy-start | bytes 884740
  737.6 2.1 copy-start.5
  740.4 2.7 copy-start.4
  743.1 1.1 copy-start.7
  743.1 1.2 copy-start.8
Sparse Core Ops, SparseCore 0:
  11.9 93.1 all-gather.1
  140.1 280.3 all-reduce.8
  455.0 282.5 all-reduce.6
where the time goes:
time: 757 us
  waiting for transfers between devices  594 us (78%)
  blocking collectives  107 us (14%)
  matrix products  26.2 us (3%)
  between operations  14 us (2%)
  local copies, waits for them, and re-layouts  13.3 us (2%)
    psum x2, waiting for transfers between devices, column_round(): attn_full, mlp_full = lax.psum((attn_term, mlp_term), ('shard', 'rep'))  561 us
    all_gather x1, blocking collectives, per_device(): lax.all_gather(attn_basis, 'shard', axis=2, tiled=True)  59.7 us
    all_gather x1, waiting for transfers between devices, per_device(): lax.all_gather(mlp_basis, 'shard', axis=2, tiled=True)  33.6 us
    psum x1, blocking collectives, per_device(): attn_first, mlp_first = lax.psum((attn_first, mlp_first), 'rep')  23.7 us
    psum x1, blocking collectives, per_device(): lax.psum((rows_product(attn_data, attn_rhat), rows_product(mlp_data, mlp_...  23.4 us
  transfers between devices with their start and end apart: 3, of which 3 were waited for; matrix products, arithmetic and copies ran while one was open for 1% of the time, Pallas kernels for 0%

commit v1 on v0

--- a/solution.py
+++ b/solution.py
@@ -5,6 +5,7 @@
 
 momentum_decay = 0.9
 learn_rate = 0.05
+_part_lanes = lambda chunk: jax.lax.psum(jax.lax.psum(chunk, "rep"), "shard")
 
 
 def rows_product(merged, factor):
@@ -34,7 +35,7 @@
 
 
 def column_round(attn_term, mlp_term, attn_roots, mlp_roots, round_index):
-    attn_full, mlp_full = lax.psum((attn_term, mlp_term), ("shard", "rep"))
+    attn_full, mlp_full = _part_lanes((attn_term, mlp_term))
     attn_full = finish(attn_full, attn_roots, round_index)
     mlp_full = finish(mlp_full, mlp_roots, round_index)
     attn_share = own_share(attn_full)

time: 757 us -> 785 us (1.037)
  waiting for transfers between devices: 594 us -> 621 us
    psum x2 -> x4, waiting for transfers between devices: 561 us -> 587 us  [the longest x2 410 us: jax.lax.psum(jax.lax.psum(chunk, 'rep'), 'shard')]
  transfers between devices with their start and end apart: 3 -> 5, of which waited for: 3 -> 5; matrix products, arithmetic and copies ran while one was open for 1% -> 1% of each run, Pallas kernels for 0% -> 0%
where the time goes in v1:
time: 785 us; the launch traced here: 784 us
  waiting for transfers between devices  621 us (79%)
  blocking collectives  108 us (14%)
  matrix products  26.2 us (3%)
  between operations  14 us (2%)
  local copies, waits for them, and re-layouts  12.9 us (2%)
    psum x2, waiting for transfers between devices, jax.lax.psum(jax.lax.psum(chunk, 'rep'), 'shard')  410 us
    psum x2, waiting for transfers between devices, jax.lax.psum(chunk, 'rep')  177 us
    all_gather x1, blocking collectives, per_device(): lax.all_gather(attn_basis, 'shard', axis=2, tiled=True)  59.7 us
    all_gather x1, waiting for transfers between devices, per_device(): lax.all_gather(mlp_basis, 'shard', axis=2, tiled=True)  33.6 us
    psum x1, blocking collectives, per_device(): lax.psum((rows_product(attn_data, attn_rhat), rows_product(mlp_data, mlp_...  24.6 us
    psum x1, blocking collectives, per_device(): attn_first, mlp_first = lax.psum((attn_first, mlp_first), 'rep')  23.7 us
  transfers between devices with their start and end apart: 5, of which 5 were waited for; matrix products, arithmetic and copies ran while one was open for 1% of the time, Pallas kernels for 0%

profile of v1, /device:TPU:1, one launch (start us, length us, event | category | flops | bytes accessed | tf_op | source)
XLA Modules:
  0.0 784.4 jit_solution(6959431743188502121)
XLA Ops:
  7.2 1.6 copy.101
  8.9 0.8 copy.94
  9.7 59.7 %all_gather.6 = f32[2,4,768,32]{3,1,0,2:T(4,128)S(1)} all-gather(f32[2,4,12,32]{3,1,0,2:T(4,128)S(1)} %copy.94), channel_id=1, replica_groups=mesh['shard'=64,'rep'=8] {'shard'}, dimensions={2}, use_global_device_ids=true | all-gather | bytes 798720 | tf_op jit(solution)/shard_map/all_gather | solution.py:75
  69.4 2.1 fusion.2
  71.6 33.6 %all-gather.2.cloned.1.call-done = f32[2,2,3072,32]{3,1,0,2:T(2,128)} async-done(((f32[2,2,48,32]{3,1,0,2:T(2,128)}), f32[2,2,3072,32]{3,1,0,2:T(2,128)}) %all-gather.2.cloned.1.call-update) | async-done | bytes 1572880 | tf_op jit(solution)/shard_map/all_gather | solution.py:76
  105.2 6.1 fusion
  111.3 23.7 %all-reduce.3 = (f32[2,4,12,32]{3,2,1,0:T(8,128)S(1)}, f32[2,2,12,32]{3,2,1,0:T(8,128)S(1)}) all-reduce(f32[2,4,12,32]{3,2,1,0:T(8,128)S(1)} %fusion.2, f32[2,2,12,32]{3,2,1,0:T(8,128)S(1)} %fusion), channel_id=1, replica_groups=mesh['shard'=64,'rep'=8] {'rep'}, use_global_device_ids=true, to_apply=%region_0.0 | all-reduce | flops 4608 | bytes 36864 | tf_op jit(solution)/shard_map/psum | solution.py:83
  135.3 1.7 fusion.17
  137.2 2.8 fusion.8
  140.1 86.9 %all-reduce.17.cloned.1.call-done = (f32[2,4,768,32]{2,3,1,0:T(8,128)}, f32[2,2,3072,32]{2,3,1,0:T(8,128)}) async-done(((f32[2,4,768,32]{2,3,1,0:T(8,128)}, f32[2,2,3072,32]{2,3,1,0:T(8,128)}), (f32[2,4,768,32]{2,3,1,0:T(8,128)}, f32[2,2,3072,32]{2,3,1,0:T(8,128)})) %all-reduce.17.cloned.1.call-update) | async-done | bytes 2359312 | tf_op jit(solution)/shard_map/psum | solution.py:8
  227.3 206.0 %all-reduce.13.cloned.1.call-done = (f32[2,4,768,32]{2,3,1,0:T(8,128)}, f32[2,2,3072,32]{2,3,1,0:T(8,128)}) async-done(((f32[2,4,768,32]{2,3,1,0:T(8,128)}, f32[2,2,3072,32]{2,3,1,0:T(8,128)}), (f32[2,4,768,32]{2,3,1,0:T(8,128)}, f32[2,2,3072,32]{2,3,1,0:T(8,128)})) %all-reduce.13.cloned.1.call-update) | async-done | bytes 2359312 | tf_op jit(solution)/shard_map/psum | solution.py:8
  433.3 2.1 fusion.22
  435.4 0.8 fusion.15
  436.2 1.5 fusion.31
  437.7 1.6 fusion.6
  439.3 24.6 %all-reduce.2 = (f32[2,4,12,32]{3,2,1,0:T(8,128)S(1)}, f32[2,2,12,32]{3,2,1,0:T(8,128)S(1)}, f32[2,156]{1,0:T(2,128)S(1)}) all-reduce(f32[2,4,12,32]{3,2,1,0:T(8,128)S(1)} %fusion.15, f32[2,2,12,32]{3,2,1,0:T(8,128)S(1)} %fusion.6, f32[2,156]{1,0:T(2,128)S(1)} %bitcast_convert_fusion), channel_id=1, replica_groups=mesh['shard'=64,'rep'=8] {'rep'}, use_global_device_ids=true, to_apply=%region_3.0 | all-reduce | flops 4920 | bytes 39360 | tf_op jit(solution)/shard_map/psum | solution.py:93
  464.3 1.7 fusion.13
  466.0 2.8 fusion.4
  469.1 89.9 %all-reduce.15.cloned.1.call-done = (f32[2,4,768,32]{2,3,1,0:T(8,128)}, f32[2,2,3072,32]{2,3,1,0:T(8,128)}) async-done(((f32[2,4,768,32]{2,3,1,0:T(8,128)}, f32[2,2,3072,32]{2,3,1,0:T(8,128)}), (f32[2,4,768,32]{2,3,1,0:T(8,128)}, f32[2,2,3072,32]{2,3,1,0:T(8,128)})) %all-reduce.15.cloned.1.call-update) | async-done | bytes 2359312 | tf_op jit(solution)/shard_map/psum | solution.py:8
  560.9 204.2 %all-reduce.11.cloned.1.call-done = (f32[2,4,768,32]{2,3,1,0:T(8,128)}, f32[2,2,3072,32]{2,3,1,0:T(8,128)}) async-done(((f32[2,4,768,32]{2,3,1,0:T(8,128)}, f32[2,2,3072,32]{2,3,1,0:T(8,128)}), (f32[2,4,768,32]{2,3,1,0:T(8,128)}, f32[2,2,3072,32]{2,3,1,0:T(8,128)})) %all-reduce.11.cloned.1.call-update) | async-done | bytes 2359312 | tf_op jit(solution)/shard_map/psum | solution.py:8
  765.0 1.3 broadcast_multiply_fusion.1
  766.4 0.7 copy.113
  767.2 0.7 copy_subtract_fusion.1
  767.9 0.9 copy.116
  768.8 0.9 copy.115
  769.7 0.9 copy.110
  770.7 0.9 copy-done.7
  771.8 1.5 copy_subtract_fusion
  773.4 1.3 copy.118
  774.6 1.3 copy.117
  775.9 1.3 copy.111
  777.2 0.7 constant_dynamic-slice_fusion
  (51 shorter events, 3.8 us)
Async XLA Ops:
  7.2 98.0 %all-gather.2.cloned.1.call-start = ((), (), s32[]{:S(2)}) async-start(), calls=%async_computation | async-start | bytes 6389760 | tf_op jit(solution)/shard_map/all_gather | solution.py:76
  8.8 218.2 %all-reduce.17.cloned.1.call-start = ((), (), s32[]{:S(2)}) async-start(), calls=%async_computation.4 | async-start | bytes 4718592 | tf_op jit(solution)/shard_map/psum | solution.py:8
  9.7 59.7 %copy-start.2 = (f32[1,2,4,12,768]{4,2,3,1,0:T(4,128)S(1)}, f32[1,2,4,12,768]{4,2,3,1,0:T(4,128)}, u32[]{:S(2)}) copy-start(f32[1,2,4,12,768]{4,2,3,1,0:T(4,128)} %param.16) | copy-start | bytes 884740
  9.7 59.7 %copy-start.3 = (bf16[1,2,4,12,768]{4,2,3,1,0:T(4,128)(2,1)S(1)}, bf16[1,2,4,12,768]{4,2,3,1,0:T(4,128)(2,1)}, u32[]{:S(2)}) copy-start(bf16[1,2,4,12,768]{4,2,3,1,0:T(4,128)(2,1)} %param.15) | copy-start | bytes 442372
  69.4 35.8 %copy-start = (f32[1,2,2,12,3072]{4,2,3,1,0:T(2,128)S(1)}, f32[1,2,2,12,3072]{4,2,3,1,0:T(2,128)}, u32[]{:S(2)}) copy-start(f32[1,2,2,12,3072]{4,2,3,1,0:T(2,128)} %param.22) | copy-start | bytes 1769476
  69.4 35.8 %copy-start.1 = (bf16[1,2,2,12,3072]{4,2,3,1,0:T(2,128)(2,1)S(1)}, bf16[1,2,2,12,3072]{4,2,3,1,0:T(2,128)(2,1)}, u32[]{:S(2)}) copy-start(bf16[1,2,2,12,3072]{4,2,3,1,0:T(2,128)(2,1)} %param.21) | copy-start | bytes 884740
  71.5 63.5 %copy-start.11 = (f32[2,4,3,32,32]{4,3,2,1,0:T(8,128)S(1)}, f32[2,4,3,32,32]{4,3,2,1,0:T(8,128)}, u32[]{:S(2)}) copy-start(f32[2,4,3,32,32]{4,3,2,1,0:T(8,128)} %param.18) | copy-start | bytes 294916
  111.3 25.7 %copy-start.12 = (f32[2,2,3,32,32]{4,3,2,1,0:T(8,128)S(1)}, f32[2,2,3,32,32]{4,3,2,1,0:T(8,128)}, u32[]{:S(2)}) copy-start(f32[2,2,3,32,32]{4,3,2,1,0:T(8,128)} %param.24) | copy-start | bytes 147460
  140.0 87.2 %copy-start.15 = (bf16[1,2,156]{2,1,0:T(2,128)(2,1)S(1)}, bf16[1,2,156]{2,1,0:T(2,128)(2,1)}, u32[]{:S(2)}) copy-start(bf16[1,2,156]{2,1,0:T(2,128)(2,1)} %param.27) | copy-start | bytes 1876
  140.0 293.3 %all-reduce.13.cloned.1.call-start = ((), (), s32[]{:S(2)}) async-start(), calls=%async_computation.2 | async-start | bytes 4718592 | tf_op jit(solution)/shard_map/psum | solution.py:8
  227.0 331.9 %all-reduce.15.cloned.1.call-start = ((), (), s32[]{:S(2)}) async-start(), calls=%async_computation.3 | async-start | bytes 4718592 | tf_op jit(solution)/shard_map/psum | solution.py:8
  433.3 2.9 copy-start.6
  468.8 91.5 %copy-start.13 = (f32[2,156]{1,0:T(2,128)S(1)}, f32[2,156]{1,0:T(2,128)}, u32[]{:S(2)}) copy-start(f32[2,156]{1,0:T(2,128)} %param.29) | copy-start | bytes 3748
  468.8 91.5 %copy-start.14 = (f32[2,156]{1,0:T(2,128)S(1)}, f32[2,156]{1,0:T(2,128)}, u32[]{:S(2)}) copy-start(f32[2,156]{1,0:T(2,128)} %param.28) | copy-start | bytes 3748
  468.8 296.2 %all-reduce.11.cloned.1.call-start = ((), (), s32[]{:S(2)}) async-start(), calls=%async_computation.1 | async-start | bytes 4718592 | tf_op jit(solution)/shard_map/psum | solution.py:8
  559.0 208.2 %copy-start.9 = (f32[2,4,12,768]{3,1,2,0:T(4,128)S(1)}, f32[2,4,12,768]{3,1,2,0:T(4,128)}, u32[]{:S(2)}) copy-start(f32[2,4,12,768]{3,1,2,0:T(4,128)} %param.20) | copy-start | bytes 884740
  559.0 208.2 %copy-start.10 = (f32[2,4,12,768]{3,1,2,0:T(4,128)S(1)}, f32[2,4,12,768]{3,1,2,0:T(4,128)}, u32[]{:S(2)}) copy-start(f32[2,4,12,768]{3,1,2,0:T(4,128)} %param.19) | copy-start | bytes 884740
  765.0 2.1 copy-start.5
  767.9 2.7 copy-start.4
  770.6 1.1 copy-start.7
  770.6 1.2 copy-start.8
Sparse Core Ops, SparseCore 0:
  11.9 93.1 all-gather.1
  140.1 86.7 all-reduce.16
  230.6 202.6 all-reduce.12
  468.9 89.9 all-reduce.14
  562.4 202.6 all-reduce.10
